TPU v7x, 32 devices: a whole 2x2x4 slice. The times are simulated.
32 devices in a mesh: dp: 8 (over y, x, core), tensor: 4 (over z).
Axes of the slice: x: 2, y: 2, z: 4, core: 2. Of those that a mesh axis runs over, the one named last changes fastest.
Arguments:
- grad_inproj: bfloat16 [8, 768, 2304], P('dp', None, 'tensor'), may hold values from -32 to 32
- error_inproj: float32 [8, 768, 2304], P('dp', None, 'tensor'), may hold values from -3 to 3
- basis_inproj: float32 [2304, 32], P('tensor'), may hold values from -6 to 6
- weight_inproj: float32 [768, 2304], P('dp', 'tensor'), may hold values from -0.3 to 0.3
- moment_inproj: float32 [768, 2304], P('dp', 'tensor'), may hold values from -0.3 to 0.3
- grad_outproj: bfloat16 [8, 768, 768], P('dp', 'tensor'), may hold values from -32 to 32
- error_outproj: float32 [8, 768, 768], P('dp', 'tensor'), may hold values from -3 to 3
- basis_outproj: float32 [768, 32], replicated, may hold values from -6 to 6
- weight_outproj: float32 [768, 768], P(('tensor', 'dp')), may hold values from -0.3 to 0.3
- moment_outproj: float32 [768, 768], P(('tensor', 'dp')), may hold values from -0.3 to 0.3
- grad_expand: bfloat16 [8, 768, 3072], P('dp', None, 'tensor'), may hold values from -32 to 32
- error_expand: float32 [8, 768, 3072], P('dp', None, 'tensor'), may hold values from -3 to 3
- basis_expand: float32 [3072, 32], P('tensor'), may hold values from -6 to 6
- weight_expand: float32 [768, 3072], P('dp', 'tensor'), may hold values from -0.3 to 0.3
- moment_expand: float32 [768, 3072], P('dp', 'tensor'), may hold values from -0.3 to 0.3
- grad_contract: bfloat16 [8, 3072, 768], P('dp', 'tensor'), may hold values from -32 to 32
- error_contract: float32 [8, 3072, 768], P('dp', 'tensor'), may hold values from -3 to 3
- basis_contract: float32 [768, 32], replicated, may hold values from -6 to 6
- weight_contract: float32 [3072, 768], P(('tensor', 'dp')), may hold values from -0.3 to 0.3
- moment_contract: float32 [3072, 768], P(('tensor', 'dp')), may hold values from -0.3 to 0.3
Outputs:
- residue_inproj: float32 [8, 768, 2304], P('dp', None, 'tensor')
- factor_inproj: float32 [2304, 32], P('tensor')
- master_inproj: float32 [768, 2304], P('dp', 'tensor')
- velocity_inproj: float32 [768, 2304], P('dp', 'tensor')
- serving_inproj: bfloat16 [768, 2304], P(None, 'tensor')
- residue_outproj: float32 [8, 768, 768], P('dp', 'tensor')
- factor_outproj: float32 [768, 32], replicated
- master_outproj: float32 [768, 768], P(('tensor', 'dp'))
- velocity_outproj: float32 [768, 768], P(('tensor', 'dp'))
- serving_outproj: bfloat16 [768, 768], P('tensor')
- residue_expand: float32 [8, 768, 3072], P('dp', None, 'tensor')
- factor_expand: float32 [3072, 32], P('tensor')
- master_expand: float32 [768, 3072], P('dp', 'tensor')
- velocity_expand: float32 [768, 3072], P('dp', 'tensor')
- serving_expand: bfloat16 [768, 3072], P(None, 'tensor')
- residue_contract: float32 [8, 3072, 768], P('dp', 'tensor')
- factor_contract: float32 [768, 32], replicated
- master_contract: float32 [3072, 768], P(('tensor', 'dp'))
- velocity_contract: float32 [3072, 768], P(('tensor', 'dp'))
- serving_contract: bfloat16 [3072, 768], P('tensor')
All inputs are finite; a program needn't handle non-finite values.
Results may differ from a plain program's by a relative error of at most 0.012.
Values may be sent and summed in bfloat16 or wider, within the bound.
A program may use at most 128 MiB of HBM per device.

v0:
```python
import jax
import jax.numpy as jnp
from jax import lax
from jax.sharding import PartitionSpec as P

NS_STEPS = 5


momentum_beta = 0.9
step_size = 0.05


def matmul_high(left, right):
    return jnp.dot(left, right, precision=lax.Precision.HIGHEST, preferred_element_type=jnp.float32)


def inverse_root(gram):
    identity = jnp.eye(gram.shape[0], dtype=jnp.float32)
    norm_total = jnp.sqrt(jnp.sum(gram * gram)) + 1e-06
    iter_y = gram / norm_total
    iter_z = identity
    for repeat in range(NS_STEPS):
        middle = 1.5 * identity - 0.5 * matmul_high(iter_z, iter_y)
        iter_y = matmul_high(iter_y, middle)
        iter_z = matmul_high(middle, iter_z)
    return iter_z / jnp.sqrt(norm_total)


def own_rows(approx, weight):
    height = weight.shape[0]
    start = lax.axis_index("dp") * height
    return lax.dynamic_slice_in_dim(approx, start, height, 0)


def pair_update(col_group, row_group):
    grad_col, error_col, basis_col, weight_col, moment_col = col_group
    grad_row, error_row, basis_row, weight_row, moment_row = row_group
    replicas = lax.axis_size("dp")
    merged_col = grad_col[0].astype(jnp.float32) + error_col[0]
    merged_row = grad_row[0].astype(jnp.float32) + error_row[0]
    part_col = matmul_high(merged_col, basis_col)
    part_row = matmul_high(merged_row, basis_row)
    left_col = lax.psum(part_col, ("dp", "tensor")) / replicas
    left_row = lax.psum(part_row, "dp") / replicas
    gram_row = lax.psum(matmul_high(left_row.T, left_row), "tensor")
    gram_col = matmul_high(left_col.T, left_col)
    normed_col = matmul_high(left_col, inverse_root(gram_col))
    normed_row = matmul_high(left_row, inverse_root(gram_row))
    factor_col = (
        lax.psum(matmul_high(merged_col.T, normed_col).astype(jnp.bfloat16), "dp").astype(
            jnp.float32
        )
        / replicas
    )
    factor_row = lax.psum(matmul_high(merged_row.T, normed_row), ("dp", "tensor")) / replicas
    approx_col = matmul_high(normed_col, factor_col.T)
    approx_row = matmul_high(normed_row, factor_row.T)
    residue_col = (merged_col - approx_col)[None]
    residue_row = (merged_row - approx_row)[None]
    velocity_col = momentum_beta * moment_col + own_rows(approx_col, weight_col)
    velocity_row = momentum_beta * moment_row + own_rows(approx_row, weight_row)
    master_col = weight_col - step_size * velocity_col
    master_row = weight_row - step_size * velocity_row
    serving_col, serving_row = (
        lax.all_gather(master_col.astype(jnp.bfloat16), "dp", axis=0, tiled=True),
        lax.all_gather(master_row.astype(jnp.bfloat16), "dp", axis=0, tiled=True),
    )
    return (
        (residue_col, factor_col, master_col, velocity_col, serving_col),
        (residue_row, factor_row, master_row, velocity_row, serving_row),
    )


def body(
    grad_inproj,
    error_inproj,
    basis_inproj,
    weight_inproj,
    moment_inproj,
    grad_outproj,
    error_outproj,
    basis_outproj,
    weight_outproj,
    moment_outproj,
    grad_expand,
    error_expand,
    basis_expand,
    weight_expand,
    moment_expand,
    grad_contract,
    error_contract,
    basis_contract,
    weight_contract,
    moment_contract,
):
    first, second = pair_update(
        (grad_inproj, error_inproj, basis_inproj, weight_inproj, moment_inproj),
        (grad_outproj, error_outproj, basis_outproj, weight_outproj, moment_outproj),
    )
    third, fourth = pair_update(
        (grad_expand, error_expand, basis_expand, weight_expand, moment_expand),
        (grad_contract, error_contract, basis_contract, weight_contract, moment_contract),
    )
    return (
        first[0],
        first[1],
        first[2],
        first[3],
        first[4],
        second[0],
        second[1],
        second[2],
        second[3],
        second[4],
        third[0],
        third[1],
        third[2],
        third[3],
        third[4],
        fourth[0],
        fourth[1],
        fourth[2],
        fourth[3],
        fourth[4],
    )


def solution(mesh):
    in_specs = (
        P("dp", None, "tensor"),
        P("dp", None, "tensor"),
        P("tensor", None),
        P("dp", "tensor"),
        P("dp", "tensor"),
        P("dp", "tensor", None),
        P("dp", "tensor", None),
        P(),
        P(("tensor", "dp"), None),
        P(("tensor", "dp"), None),
        P("dp", None, "tensor"),
        P("dp", None, "tensor"),
        P("tensor", None),
        P("dp", "tensor"),
        P("dp", "tensor"),
        P("dp", "tensor", None),
        P("dp", "tensor", None),
        P(),
        P(("tensor", "dp"), None),
        P(("tensor", "dp"), None),
    )
    out_specs = (
        P("dp", None, "tensor"),
        P("tensor", None),
        P("dp", "tensor"),
        P("dp", "tensor"),
        P(None, "tensor"),
        P("dp", "tensor", None),
        P(),
        P(("tensor", "dp"), None),
        P(("tensor", "dp"), None),
        P("tensor", None),
        P("dp", None, "tensor"),
        P("tensor", None),
        P("dp", "tensor"),
        P("dp", "tensor"),
        P(None, "tensor"),
        P("dp", "tensor", None),
        P(),
        P(("tensor", "dp"), None),
        P(("tensor", "dp"), None),
        P("tensor", None),
    )
    return jax.shard_map(body, mesh=mesh, in_specs=in_specs, out_specs=out_specs, check_vma=False)
```

profile of v0, /device:TPU:0, one launch (start us, length us, event | category | flops | bytes accessed | tf_op | source)
XLA Modules:
  0.0 365.6 jit_solution(10655994586328658243)
XLA Ops:
  8.1 5.1 %fusion.2 = f32[768,32]{0,1:T(8,128)} fusion(f32[768,32]{0,1:T(8,128)S(1)} %copy-done, f32[1,768,768]{2,1,0:T(8,128)} %param.36, bf16[1,768,768]{2,1,0:T(8,128)(2,1)} %param.35), kind=kOutput, calls=%fused_computation.3 | convolution fusion | flops 227672064 | bytes 3735552 | tf_op jit(solution)/shard_map/dot_general | solution.py:14
  13.3 1.6 fusion.43
  14.9 25.5 %psum.72 = f32[192,32]{0,1:T(8,128)S(1)} all-reduce(f32[192,32]{0,1:T(8,128)S(1)} %fusion.43), channel_id=1, replica_groups=mesh['dp'=8,'tensor'=4] {'dp'}, use_global_device_ids=true, to_apply=%region_3.0 | all-reduce | flops 6144 | bytes 49152 | tf_op jit(solution)/shard_map/psum | solution.py:44
  40.4 1.9 fusion.12
  42.3 5.1 %fusion.7 = f32[768,32]{0,1:T(8,128)} fusion(f32[768,32]{0,1:T(8,128)} %param.32, f32[1,768,768]{2,1,0:T(8,128)} %param.31, bf16[1,768,768]{2,1,0:T(8,128)(2,1)} %param.30), kind=kOutput, calls=%fused_computation.9 | convolution fusion | flops 227672064 | bytes 3735552 | tf_op jit(solution)/shard_map/dot_general | solution.py:14
  47.6 20.0 %all-reduce.7.cloned.1.call-done = f32[768,32]{0,1:T(8,128)} async-done(((f32[768,32]{0,1:T(8,128)}), f32[768,32]{0,1:T(8,128)}) %all-reduce.7.cloned.1.call-update) | async-done | bytes 98320 | tf_op jit(solution)/shard_map/psum | solution.py:44
  68.8 19.0 %all-reduce.1 = (f32[32,32]{1,0:T(8,128)S(1)}, f32[32,32]{1,0:T(8,128)S(1)}) all-reduce(f32[32,32]{1,0:T(8,128)S(1)} %fusion.66, f32[32,32]{1,0:T(8,128)S(1)} %fusion.48), channel_id=1, replica_groups=mesh['dp'=8,'tensor'=4] {'tensor'}, use_global_device_ids=true, to_apply=%region_4.0 | all-reduce | flops 2048 | bytes 16384 | tf_op jit(solution)/shard_map/psum | solution.py:45
  95.0 3.5 fusion
  101.1 126.5 %all-reduce.9.cloned.1.call-done = (f32[768,32]{0,1:T(8,128)}, f32[768,32]{0,1:T(8,128)}, f32[768,32]{0,1:T(8,128)}, f32[768,32]{0,1:T(8,128)}) async-done(((f32[768,32]{0,1:T(8,128)}, f32[768,32]{0,1:T(8,128)}, f32[768,32]{0,1:T(8,128)}, f32[768,32]{0,1:T(8,128)}), (f32[768,32]{0,1:T(8,128)}, f32[768,32]{0,1:T(8,128)}, f32[768,32]{0,1:T(8,128)}, f32[768,32]{0,1:T(8,128)})) %all-reduce.9.cloned.1.call-update) | async-done | bytes 393232 | tf_op jit(solution)/shard_map/psum | solution.py:43
  227.6 1.8 multiply_reduce_fusion.1
  231.9 1.8 multiply_reduce_fusion.3
  236.6 1.3 fusion.50
  237.9 4.3 %fusion.15 = bf16[768,32]{0,1:T(8,128)(2,1)} fusion(f32[768,32]{0,1:T(8,128)S(1)} %fusion.50, f32[1,768,768]{2,1,0:T(8,128)} %param.31, bf16[1,768,768]{2,1,0:T(8,128)(2,1)} %param.30), kind=kOutput, calls=%fused_computation.21 | convolution fusion | flops 227696640 | bytes 3686400 | tf_op jit(solution)/shard_map/dot_general | solution.py:14
  243.7 2.3 fusion.18
  247.5 3.5 fusion.117
  251.1 2.1 fusion.86
  253.2 1.8 copy.44
  255.0 1.8 copy.45
  257.7 1.5 fusion.103
  260.0 1.6 fusion.88
  261.6 3.8 %fusion.4 = f32[1,768,768]{2,1,0:T(8,128)} fusion(f32[768,768]{1,0:T(8,128)} %fusion.117, f32[1,768,768]{2,1,0:T(8,128)S(1)} %copy-done.1, bf16[1,768,768]{2,1,0:T(8,128)(2,1)} %param.35), kind=kLoop, calls=%fused_computation.5 | loop fusion | flops 1769472 | bytes 8257536 | tf_op jit(solution)/shard_map/broadcast_in_dim | solution.py:59
  265.4 35.7 %all-reduce.11.cloned.1.call-done = (bf16[576,32]{0,1:T(8,128)(2,1)}, bf16[768,32]{0,1:T(8,128)(2,1)}) async-done(((bf16[576,32]{0,1:T(8,128)(2,1)}, bf16[768,32]{0,1:T(8,128)(2,1)}), (bf16[576,32]{0,1:T(8,128)(2,1)}, bf16[768,32]{0,1:T(8,128)(2,1)})) %all-reduce.11.cloned.1.call-update) | async-done | bytes 86032 | tf_op jit(solution)/shard_map/psum | solution.py:50
  302.7 2.1 fusion.110
  305.9 11.7 %all_gather.13 = bf16[192,768]{1,0:T(8,128)(2,1)} all-gather(bf16[24,768]{1,0:T(8,128)(2,1)} %get-tuple-element.74), channel_id=1, replica_groups=mesh['dp'=8,'tensor'=4] {'dp'}, dimensions={0}, use_global_device_ids=true | all-gather | bytes 331776 | tf_op jit(solution)/shard_map/all_gather | solution.py:66
  317.6 2.2 fusion.45
  321.2 1.6 fusion.96
  324.4 10.8 %all_gather.12 = bf16[768,576]{1,0:T(8,128)(2,1)S(1)} all-gather(bf16[96,576]{1,0:T(8,128)(2,1)S(1)} %copy.46), channel_id=1, replica_groups=mesh['dp'=8,'tensor'=4] {'dp'}, dimensions={0}, use_global_device_ids=true | all-gather | bytes 995328 | tf_op jit(solution)/shard_map/all_gather | solution.py:65
  335.2 1.3 copy.49
  338.2 3.7 %fusion.14 = f32[1,768,576]{1,2,0:T(8,128)} fusion(f32[768,576]{0,1:T(8,128)} %copy-done.8, f32[1,768,576]{1,2,0:T(8,128)} %param.21, bf16[1,768,576]{1,2,0:T(8,128)(2,1)S(1)} %copy-done.9), kind=kLoop, calls=%fused_computation.19 | loop fusion | flops 1327104 | bytes 6193152 | tf_op jit(solution)/shard_map/broadcast_in_dim | solution.py:58
  342.6 1.8 fusion.9
  344.4 10.6 %all-gather.3.cloned.1.call-done = bf16[768,768]{1,0:T(8,128)(2,1)} async-done(((bf16[96,768]{1,0:T(8,128)(2,1)}), bf16[768,768]{1,0:T(8,128)(2,1)}) %all-gather.3.cloned.1.call-update) | async-done | bytes 1179664 | tf_op jit(solution)/shard_map/all_gather | solution.py:65
  355.7 2.4 copy.61
  (147 shorter events, 28.7 us)
Async XLA Ops:
  7.2 0.9 copy-start
  7.2 6.1 %copy-start.10 = (f32[1,192,768]{2,1,0:T(8,128)S(1)}, f32[1,192,768]{2,1,0:T(8,128)}, u32[]{:S(2)}) copy-start(f32[1,192,768]{2,1,0:T(8,128)} %param.26) | copy-start | bytes 1769476
  7.2 6.1 %copy-start.29 = (f32[768,32]{0,1:T(8,128)S(1)}, f32[768,32]{0,1:T(8,128)}, u32[]{:S(2)}) copy-start(f32[768,32]{0,1:T(8,128)} %param.27) | copy-start | bytes 294916
  7.2 33.2 %copy-start.9 = (bf16[1,768,576]{1,2,0:T(8,128)(2,1)S(1)}, bf16[1,768,576]{1,2,0:T(8,128)(2,1)}, u32[]{:S(2)}) copy-start(bf16[1,768,576]{1,2,0:T(8,128)(2,1)} %param.20) | copy-start | bytes 2654212
  7.2 33.2 %copy-start.3 = (f32[1,768,576]{1,2,0:T(8,128)S(1)}, f32[1,768,576]{1,2,0:T(8,128)}, u32[]{:S(2)}) copy-start(f32[1,768,576]{1,2,0:T(8,128)} %param.21) | copy-start | bytes 5308420
  7.3 33.2 %copy-start.30 = (f32[576,32]{0,1:T(8,128)S(1)}, f32[576,32]{0,1:T(8,128)}, u32[]{:S(2)}) copy-start(f32[576,32]{0,1:T(8,128)} %param.22) | copy-start | bytes 221188
  7.3 60.3 %all-reduce.7.cloned.1.call-start = ((), (), s32[]{:S(2)}) async-start(), calls=%async_computation.1 | async-start | bytes 196608 | tf_op jit(solution)/shard_map/psum | solution.py:44
  13.2 214.3 %all-reduce.9.cloned.1.call-start = ((), (), s32[]{:S(2)}) async-start(), calls=%async_computation.3 | async-start | bytes 786432 | tf_op jit(solution)/shard_map/psum | solution.py:43
  42.3 52.7 %copy-start.1 = (f32[1,768,768]{2,1,0:T(8,128)S(1)}, f32[1,768,768]{2,1,0:T(8,128)}, u32[]{:S(2)}) copy-start(f32[1,768,768]{2,1,0:T(8,128)} %param.36) | copy-start | bytes 7077892
  93.5 6.2 %copy-start.11 = (f32[1,192,768]{2,1,0:T(8,128)S(1)}, f32[1,192,768]{2,1,0:T(8,128)}, u32[]{:S(2)}) copy-start(f32[1,192,768]{2,1,0:T(8,128)} %param.26) | copy-start | bytes 1769476
  93.5 6.2 %copy-start.13 = (bf16[1,192,768]{2,1,0:T(8,128)(2,1)S(1)}, bf16[1,192,768]{2,1,0:T(8,128)(2,1)}, u32[]{:S(2)}) copy-start(bf16[1,192,768]{2,1,0:T(8,128)(2,1)} %param.25) | copy-start | bytes 884740
  100.9 200.3 %all-reduce.11.cloned.1.call-start = ((), (), s32[]{:S(2)}) async-start(), calls=%async_computation.4 | async-start | bytes 180224 | tf_op jit(solution)/shard_map/psum | solution.py:50
  236.3 7.4 %copy-start.4 = (f32[1,768,576]{1,2,0:T(8,128)S(1)}, f32[1,768,576]{1,2,0:T(8,128)}, u32[]{:S(2)}) copy-start(f32[1,768,576]{1,2,0:T(8,128)} %param.21) | copy-start | bytes 5308420
  237.9 4.4 %copy-start.20 = (f32[768,32]{0,1:T(8,128)}, f32[768,32]{0,1:T(8,128)S(1)}, u32[]{:S(2)}) copy-start(f32[768,32]{0,1:T(8,128)S(1)} %fusion.50) | copy-start | bytes 294916
  251.0 93.3 %all-gather.5.cloned.1.call-start = ((), (), s32[]{:S(2)}) async-start(), calls=%async_computation.2 | async-start | bytes 1327104 | tf_op jit(solution)/shard_map/all_gather | solution.py:66
  253.2 101.9 %all-gather.3.cloned.1.call-start = ((), (), s32[]{:S(2)}) async-start(), calls=%async_computation | async-start | bytes 1327104 | tf_op jit(solution)/shard_map/all_gather | solution.py:65
  257.7 1.5 copy-start.24
  259.2 0.8 copy-start.12
  261.6 41.0 %copy-start.21 = (f32[768,32]{0,1:T(8,128)S(1)}, f32[768,32]{0,1:T(8,128)}, u32[]{:S(2)}) copy-start(f32[768,32]{0,1:T(8,128)} %copy-done.20) | copy-start | bytes 294916
  301.2 3.6 copy-start.27
  301.2 3.6 copy-start.28
  304.8 18.1 %copy-start.5 = (f32[768,768]{1,0:T(8,128)}, f32[768,768]{1,0:T(8,128)S(1)}, u32[]{:S(2)}) copy-start(f32[768,768]{1,0:T(8,128)S(1)} %fusion.110) | copy-start | bytes 7077892
  305.9 17.0 %copy-start.16 = (f32[96,576]{0,1:T(8,128)S(1)}, f32[96,576]{0,1:T(8,128)}, u32[]{:S(2)}) copy-start(f32[96,576]{0,1:T(8,128)} %copy.44) | copy-start | bytes 663556
  305.9 17.0 %copy-start.17 = (f32[96,576]{0,1:T(8,128)S(1)}, f32[96,576]{0,1:T(8,128)}, u32[]{:S(2)}) copy-start(f32[96,576]{0,1:T(8,128)} %copy.45) | copy-start | bytes 663556
  322.9 1.4 copy-start.8
  324.3 12.2 %copy-start.19 = (f32[96,576]{0,1:T(8,128)S(1)}, f32[96,576]{0,1:T(8,128)}, u32[]{:S(2)}) copy-start(f32[96,576]{0,1:T(8,128)} %get-tuple-element.78) | copy-start | bytes 663556
  324.3 13.0 %copy-start.18 = (f32[96,576]{0,1:T(8,128)S(1)}, f32[96,576]{0,1:T(8,128)}, u32[]{:S(2)}) copy-start(f32[96,576]{0,1:T(8,128)} %get-tuple-element.79) | copy-start | bytes 663556
  338.2 3.7 %copy-start.2 = (f32[1,768,768]{2,1,0:T(8,128)S(1)}, f32[1,768,768]{2,1,0:T(8,128)}, u32[]{:S(2)}) copy-start(f32[1,768,768]{2,1,0:T(8,128)} %param.31) | copy-start | bytes 7077892
  338.2 3.7 %copy-start.6 = (f32[768,768]{1,0:T(8,128)S(1)}, f32[768,768]{1,0:T(8,128)}, u32[]{:S(2)}) copy-start(f32[768,768]{1,0:T(8,128)} %copy-done.5) | copy-start | bytes 7077892
  338.2 4.4 %copy-start.7 = (bf16[1,768,768]{2,1,0:T(8,128)(2,1)S(1)}, bf16[1,768,768]{2,1,0:T(8,128)(2,1)}, u32[]{:S(2)}) copy-start(bf16[1,768,768]{2,1,0:T(8,128)(2,1)} %param.30) | copy-start | bytes 3538948
  342.6 12.4 %copy-start.15 = (bf16[192,768]{1,0:T(8,128)(2,1)S(1)}, bf16[192,768]{1,0:T(8,128)(2,1)}, u32[]{:S(2)}) copy-start(bf16[192,768]{1,0:T(8,128)(2,1)} %all_gather.13) | copy-start | bytes 884740
  344.4 13.7 %copy-start.14 = (bf16[768,768]{1,0:T(8,128)(2,1)S(1)}, bf16[768,768]{1,0:T(8,128)(2,1)}, u32[]{:S(2)}) copy-start(bf16[768,768]{1,0:T(8,128)(2,1)} %all-gather.5.cloned.1.call-done) | copy-start | bytes 3538948
  (4 other events, 2.5 us)
Sparse Core Ops, SparseCore 0:
  13.3 54.1 all-reduce.6
  101.0 126.5 all-reduce.8
  251.1 49.9 all-reduce.10
  303.1 25.3 all-gather.4
  330.9 24.0 all-gather.2
where the time goes:
time: 367 us; the launch traced here: 366 us
  waiting for transfers between devices  193 us (53%)
  blocking collectives  67 us (18%)
  matrix products  50.5 us (14%)
  other arithmetic  21.4 us (6%)
  between operations  17.4 us (5%)
  local copies, waits for them, and re-layouts  16.1 us (4%)
    psum x1, waiting for transfers between devices, pair_update(): left_col = lax.psum(part_col, ('dp', 'tensor')) / replicas  126 us
    dot_general x76, matrix products, matmul_high(): jnp.dot(left, right, precision=lax.Precision.HIGHEST, preferred_element_t...  50.5 us
    psum x1, waiting for transfers between devices, pair_update(): lax.psum(matmul_high(merged_col.T, normed_col).astype(jnp.bfloat16), 'dp')  35.7 us
    psum x1, blocking collectives, pair_update(): left_row = lax.psum(part_row, 'dp') / replicas  25.5 us
    psum x1, waiting for transfers between devices, pair_update(): left_row = lax.psum(part_row, 'dp') / replicas  20 us
    psum x1, blocking collectives, pair_update(): gram_row = lax.psum(matmul_high(left_row.T, left_row), 'tensor')  19 us
    unnamed x70, local copies, waits for them, and re-layouts  15.9 us
    all_gather x1, blocking collectives, pair_update(): lax.all_gather(master_row.astype(jnp.bfloat16), 'dp', axis=0, tiled=True)  11.7 us
  transfers between devices with their start and end apart: 5, of which 4 were waited for; matrix products, arithmetic and copies ran while one was open for 11% of the time, Pallas kernels for 0%

commit v1 on v0

v1 whole, which is shorter than its diff:
```python
import functools

import jax
import jax.numpy as jnp
from jax import lax
from jax.experimental import pallas as pl
from jax.experimental.pallas import tpu as pltpu
from jax.sharding import PartitionSpec as P

NS_STEPS = 5
RANK = 32
COUNT = 4
LANES = RANK * COUNT
COLS = 2 * RANK

momentum_beta = 0.9
step_size = 0.05

MESH = pl.DeviceIdType.MESH
F32 = jnp.float32
BF16 = jnp.bfloat16
HIGHEST = lax.Precision.HIGHEST


def dot_high(a, b, dims=(((1,), (0,)), ((), ()))):
    return lax.dot_general(a, b, dims, precision=HIGHEST, preferred_element_type=F32)


def lane_block(shape, dim):
    return lax.broadcasted_iota(jnp.int32, shape, dim) // RANK


def compact_gram(chunk):
    gram = dot_high(chunk, chunk, (((0,), (0,)), ((), ())))
    block = lane_block((RANK, LANES), 1)
    total = jnp.zeros((RANK, LANES), F32)
    for b in range(COUNT):
        total = total + jnp.where(block == b, gram[b * RANK:(b + 1) * RANK, :], 0.0)
    return total


def inverse_root(compact):
    same = lane_block((LANES, LANES), 0) == lane_block((LANES, LANES), 1)
    gram = jnp.where(same, jnp.concatenate([compact] * COUNT, axis=0), 0.0)
    identity = jnp.where(
        lax.broadcasted_iota(jnp.int32, (LANES, LANES), 0)
        == lax.broadcasted_iota(jnp.int32, (LANES, LANES), 1), 1.0, 0.0)
    squares = jnp.sum(compact * compact, axis=0, keepdims=True)
    block = lane_block((1, LANES), 1)
    norm = jnp.zeros((1, LANES), F32)
    for b in range(COUNT):
        part = jnp.sum(jnp.where(block == b, squares, 0.0), axis=1, keepdims=True)
        norm = jnp.where(block == b, part, norm)
    norm = jnp.sqrt(norm) + 1e-06
    iter_y = gram / norm
    iter_z = identity
    for repeat in range(NS_STEPS):
        zy = iter_y if repeat == 0 else dot_high(iter_z, iter_y)
        middle = 1.5 * identity - 0.5 * zy
        if repeat < NS_STEPS - 1:
            iter_y = dot_high(iter_y, middle)
        iter_z = middle if repeat == 0 else dot_high(middle, iter_z)
    return iter_z / jnp.sqrt(norm)


def split(x):
    hi = x.astype(BF16)
    return hi, (x - hi.astype(F32)).astype(BF16)


def factors_kernel(n, t, *refs):
    grads, errors, bases = refs[0:4], refs[4:8], refs[8:12]
    normed_ref, normed_out_ref, factor_ref = refs[12:15]
    gbuf, ebuf, merged, rhs = refs[15:19], refs[19:23], refs[23:27], refs[27]
    part, recv_part, cross, gathered = refs[28:32]
    fpart, recv_f, cross_f = refs[32:35]
    in_sem, s1, r1, s2, r2, s3, r3, s4, r4, s5, r5, s6, r6 = refs[35:48]

    me = lax.axis_index("dp")
    my_t = lax.axis_index("tensor")
    rows, width = part.shape[0], fpart.shape[1]
    h = rows // n
    rc = recv_f.shape[1]
    w = recv_f.shape[2]
    pieces = width // w

    loads = []
    for j in range(COUNT):
        pair = (
            pltpu.make_async_copy(grads[j].at[0], gbuf[j], in_sem.at[2 * j]),
            pltpu.make_async_copy(errors[j].at[0], ebuf[j], in_sem.at[2 * j + 1]),
        )
        for copy in pair:
            copy.start()
        loads.append(pair)

    barrier = pltpu.get_barrier_semaphore()
    for d in range(1, n):
        pl.semaphore_signal(barrier, inc=1, device_id={"dp": lax.rem(me + d, n)}, device_id_type=MESH)
    for d in range(1, t):
        pl.semaphore_signal(barrier, inc=1, device_id={"tensor": lax.rem(my_t + d, t)}, device_id_type=MESH)

    def exchange(axis, size, index, source, target, send, recv):
        out = []
        for d in range(1, size):
            peer = lax.rem(index + d, size)
            copy = pltpu.make_async_remote_copy(
                src_ref=source(peer), dst_ref=target(d), send_sem=send.at[d - 1], recv_sem=recv.at[d - 1],
                device_id={axis: peer}, device_id_type=MESH)
            copy.start()
            out.append(copy)
        return out

    def rows_of(peer):
        return pl.ds(pl.multiple_of(peer * h, 8), h)

    def piece_of(peer):
        if pieces == 1:
            return (pl.ds(pl.multiple_of(peer * rc, 8), rc), slice(None))
        return (pl.ds(pl.multiple_of((peer // pieces) * rc, 8), rc),
                pl.ds(pl.multiple_of(lax.rem(peer, pieces) * w, 128), w))

    part[...] = jnp.zeros_like(part)
    for j in range(COUNT):
        depth = bases[j].shape[0]
        columns = [jnp.zeros((depth, RANK), F32)] * COUNT
        columns[j] = bases[j][...]
        hi, lo = split(jnp.concatenate(columns, axis=1))
        rhs[0:depth, 0:LANES] = hi
        rhs[0:depth, LANES:2 * LANES] = lo
        for copy in loads[j]:
            copy.wait()
        height = gbuf[j].shape[0]
        step = min(height, 192)

        def block(i, carry, j=j, step=step, depth=depth):
            at = pl.ds(pl.multiple_of(i * step, 16), step)
            value = (gbuf[j][at, :].astype(F32) + ebuf[j][at, :]).astype(BF16)
            merged[j][at, :] = value
            both = jnp.dot(value, rhs[0:depth, :], preferred_element_type=F32)
            part[at, :] += both[:, :LANES] + both[:, LANES:]
            return carry

        lax.fori_loop(0, height // step, block, 0)

    pl.semaphore_wait(barrier, n - 1 + t - 1)

    first = exchange("dp", n, me, lambda p: part.at[rows_of(p), :], lambda d: recv_part.at[d - 1], s1, r1)
    chunk = part[rows_of(me), :]
    for d in range(1, n):
        first[d - 1].wait_recv()
        chunk = chunk + recv_part[d - 1]
    chunk = chunk / n
    cross[my_t, 0:h, :] = chunk
    cross[my_t, h:h + RANK, :] = compact_gram(chunk)
    second = exchange("tensor", t, my_t, lambda p: cross.at[my_t], lambda d: cross.at[my_t], s2, r2)
    for copy in second:
        copy.wait_recv()
    total = cross[0]
    for k in range(1, t):
        total = total + cross[k]
    col_lane = lax.broadcasted_iota(jnp.int32, (1, LANES), 1) < COLS
    mine = jnp.where(col_lane, total[0:h, :], chunk)
    gathered[me, 0:h, :] = mine
    gathered[me, h:h + RANK, :] = jnp.where(col_lane, compact_gram(mine), total[h:h + RANK, :])
    third = exchange("dp", n, me, lambda p: gathered.at[me], lambda d: gathered.at[me], s3, r3)
    for copy in third:
        copy.wait_recv()
    compact = gathered[0, h:h + RANK, :]
    for k in range(1, n):
        compact = compact + gathered[k, h:h + RANK, :]
    root = inverse_root(compact)
    left = gathered[:, 0:h, :].reshape(rows, LANES)
    normed = dot_high(left, root)
    hi, lo = split(normed)
    normed_ref[:, 0:LANES] = hi
    normed_ref[:, LANES:2 * LANES] = lo
    out_rows = normed_out_ref.shape[0]
    normed_out_ref[:, 0:LANES] = hi[0:out_rows]
    normed_out_ref[:, LANES:2 * LANES] = lo[0:out_rows]
    flipped_hi, flipped_lo = split(normed.T)

    fpart[...] = jnp.zeros_like(fpart)
    for j in range(COUNT):
        height, depth = merged[j].shape
        both = jnp.concatenate(
            [flipped_hi[j * RANK:(j + 1) * RANK, 0:height], flipped_lo[j * RANK:(j + 1) * RANK, 0:height]], axis=0)
        term = jnp.dot(both, merged[j][...], preferred_element_type=F32)
        fpart[j * RANK:(j + 1) * RANK, 0:depth] = term[0:RANK] + term[RANK:]

    fourth = exchange("dp", n, me, lambda p: fpart.at[piece_of(p)], lambda d: recv_f.at[d - 1], s4, r4)
    piece = fpart[piece_of(me)]
    for d in range(1, n):
        fourth[d - 1].wait_recv()
        piece = piece + recv_f[d - 1]
    piece = piece / n
    cross_f[my_t] = piece
    fifth = exchange("tensor", t, my_t, lambda p: cross_f.at[my_t], lambda d: cross_f.at[my_t], s5, r5)
    for copy in fifth:
        copy.wait_recv()
    total_f = cross_f[0]
    for k in range(1, t):
        total_f = total_f + cross_f[k]
    row_part = (me // pieces) * rc >= COLS
    factor_ref[piece_of(me)] = jnp.where(row_part, total_f, piece)
    sixth = exchange("dp", n, me, lambda p: factor_ref.at[piece_of(me)], lambda d: factor_ref.at[piece_of(me)], s6, r6)
    for copy in sixth:
        copy.wait_recv()
    for group in (first, second, third, fourth, fifth, sixth):
        for copy in group:
            copy.wait_send()


def factors(n, t, grads, errors, bases):
    rows = max(g.shape[1] for g in grads)
    width = max(g.shape[2] for g in grads)
    h = rows // n
    rc = max(8, LANES // n)
    pieces = n * rc // LANES
    w = width // pieces
    out_rows = grads[2].shape[1]
    dma = pltpu.SemaphoreType.DMA
    scratch = [pltpu.VMEM(g.shape[1:], BF16) for g in grads]
    scratch += [pltpu.VMEM(g.shape[1:], F32) for g in grads]
    scratch += [pltpu.VMEM(g.shape[1:], BF16) for g in grads]
    scratch += [
        pltpu.VMEM((width, 2 * LANES), BF16),
        pltpu.VMEM((rows, LANES), F32),
        pltpu.VMEM((n - 1, h, LANES), F32),
        pltpu.VMEM((t, h + RANK, LANES), F32),
        pltpu.VMEM((n, h + RANK, LANES), F32),
        pltpu.VMEM((LANES, width), F32),
        pltpu.VMEM((n - 1, rc, w), F32),
        pltpu.VMEM((t, rc, w), F32),
        dma((2 * COUNT,)),
    ]
    for size in (n, t, n, n, t, n):
        scratch += [dma((size - 1,)), dma((size - 1,))]
    return pl.pallas_call(
        functools.partial(factors_kernel, n, t),
        out_shape=(
            jax.ShapeDtypeStruct((rows, 2 * LANES), BF16),
            jax.ShapeDtypeStruct((out_rows, 2 * LANES), BF16),
            jax.ShapeDtypeStruct((LANES, width), F32),
        ),
        in_specs=[pl.BlockSpec(memory_space=pl.ANY)] * 8 + [pl.BlockSpec(memory_space=pltpu.VMEM)] * 4,
        out_specs=[pl.BlockSpec(memory_space=pltpu.VMEM)] * 3,
        scratch_shapes=scratch,
        compiler_params=pltpu.CompilerParams(
            collective_id=0, has_side_effects=True, vmem_limit_bytes=40 * 1024 * 1024),
        cost_estimate=pl.CostEstimate(flops=4_000_000_000, bytes_accessed=60_000_000, transcendentals=0),
        name="factors",
    )(*grads, *errors, *bases)


def update_kernel(*refs):
    normed, normed_out, factor = refs[0:3]
    ins, outs, rhs = refs[3:23], refs[23:39], refs[39]
    i = pl.program_id(0)
    me = lax.axis_index("dp")

    @pl.when(i == 0)
    def _():
        value = factor[...].astype(BF16)
        block = lane_block(value.shape, 0)
        for j in range(COUNT):
            masked = jnp.where(block == j, value, jnp.zeros_like(value))
            rhs[j, 0:LANES, :] = masked
            rhs[j, LANES:2 * LANES, :] = masked

    for j in range(COUNT):
        grad, error, weight, moment, early = ins[5 * j:5 * j + 5]
        residue, master, velocity, serving = outs[4 * j:4 * j + 4]
        width = grad.shape[2]
        lhs = normed_out[0] if j == 2 else normed[0]
        approx = jnp.dot(lhs, rhs[j, :, 0:width], preferred_element_type=F32)
        residue[0] = grad[0].astype(F32) + error[0] - approx
        serving[0] = (early[0].astype(F32) - step_size * approx).astype(BF16)

        @pl.when(i == me)
        def _(weight=weight, moment=moment, master=master, velocity=velocity, approx=approx):
            value = momentum_beta * moment[...] + approx
            velocity[...] = value
            master[...] = weight[...] - step_size * value


def update(n, normed, normed_out, factor, groups):
    def blocked(x, width=None):
        x = x.reshape(n, -1, x.shape[-1])
        return x, pl.BlockSpec((1,) + x.shape[1:], lambda i: (i, 0, 0))

    def whole(shape):
        return pl.BlockSpec(shape, lambda i: (0, 0))

    args, specs, out_shapes, out_specs = [], [], [], []
    for x in (normed, normed_out):
        x, spec = blocked(x)
        args.append(x)
        specs.append(spec)
    args.append(factor)
    specs.append(whole(factor.shape))
    for grad, error, weight, moment, early in groups:
        shapes = []
        for x in (grad, error):
            x, spec = blocked(x)
            args.append(x)
            specs.append(spec)
        blocks = x.shape
        args += [weight, moment]
        specs += [whole(weight.shape)] * 2
        x, spec = blocked(early)
        args.append(x)
        specs.append(spec)
        out_shapes += [jax.ShapeDtypeStruct(blocks, F32), jax.ShapeDtypeStruct(weight.shape, F32),
                       jax.ShapeDtypeStruct(weight.shape, F32), jax.ShapeDtypeStruct(blocks, BF16)]
        out_specs += [spec, whole(weight.shape), whole(weight.shape), spec]
    return pl.pallas_call(
        update_kernel,
        grid=(n,),
        out_shape=out_shapes,
        in_specs=specs,
        out_specs=out_specs,
        scratch_shapes=[pltpu.VMEM((COUNT, 2 * LANES, factor.shape[1]), BF16)],
        compiler_params=pltpu.CompilerParams(vmem_limit_bytes=40 * 1024 * 1024),
        name="update",
    )(*args)


def body(n, t, *args):
    inproj, outproj, expand, contract = (args[5 * k:5 * k + 5] for k in range(COUNT))
    order = (inproj, expand, outproj, contract)
    early = [
        lax.all_gather((w - step_size * momentum_beta * m).astype(BF16), "dp", axis=0, tiled=False)
        for _, _, _, w, m in order
    ]
    normed, normed_out, factor = factors(
        n, t, [g[0] for g in order], [g[1] for g in order], [g[2] for g in order])
    results = update(n, normed, normed_out, factor,
                     [(g[0], g[1], g[3], g[4], u) for g, u in zip(order, early)])
    outs = []
    for j in (0, 2, 1, 3):
        grad = order[j][0]
        height, width = grad.shape[1:]
        residue, master, velocity, serving = results[4 * j:4 * j + 4]
        outs += [residue.reshape(grad.shape), factor[j * RANK:(j + 1) * RANK, 0:width].T,
                 master, velocity, serving.reshape(height, width)]
    return tuple(outs)


def solution(mesh):
    col = (P("dp", None, "tensor"), P("dp", None, "tensor"), P("tensor", None), P("dp", "tensor"), P("dp", "tensor"))
    row = (P("dp", "tensor", None), P("dp", "tensor", None), P(), P(("tensor", "dp"), None), P(("tensor", "dp"), None))
    col_out = (P("dp", None, "tensor"), P("tensor", None), P("dp", "tensor"), P("dp", "tensor"), P(None, "tensor"))
    row_out = (P("dp", "tensor", None), P(), P(("tensor", "dp"), None), P(("tensor", "dp"), None), P("tensor", None))
    return jax.shard_map(
        functools.partial(body, mesh.shape["dp"], mesh.shape["tensor"]), mesh=mesh,
        in_specs=col + row + col + row, out_specs=col_out + row_out + col_out + row_out, check_vma=False)
```

time: 367 us -> 150 us (0.41)
  waiting for transfers between devices: 193 us -> 0.04 us
  Pallas kernels: 0 us -> 61.8 us
  matrix products: 50.5 us -> 0 us
  blocking collectives: 67 us -> 24.7 us
  local copies, waits for them, and re-layouts: 16.1 us -> 43.3 us
  other arithmetic: 21.4 us -> 4.58 us
    psum x3 -> x0, waiting for transfers between devices: 182 us -> none  [the longest x1 126 us: pair_update(): left_col = lax.psum(part_col, ('dp', 'tensor')) / replicas]
    pallas_call x0 -> x2, Pallas kernels: none -> 61.8 us  [the longest x1 49.8 us: factors(): pl.pallas_call(functools.partial(factors_kernel, n, t), out_shape=(jax.Sh...]
    dot_general x76 -> x0, matrix products: 50.5 us -> none  [matmul_high(): jnp.dot(left, right, precision=lax.Precision.HIGHEST, preferred_element_t...]
    psum x2 -> x0, blocking collectives: 44.5 us -> none  [the longest x1 25.5 us: pair_update(): left_row = lax.psum(part_row, 'dp') / replicas]
    unnamed x70 -> x78, local copies, waits for them, and re-layouts: 15.9 us -> 41.9 us
    broadcast_in_dim x4 -> x0, other arithmetic: 11.5 us -> none  [the longest x2 6.02 us: pair_update(): residue_row = (merged_row - approx_row)[None]]
    all_gather x2, waiting for transfers between devices: 10.6 us -> 0.01 us  [body(): lax.all_gather((w - step_size * momentum_beta * m).astype(BF16), 'dp', ax...]
  transfers between devices with their start and end apart: 5 -> 2, of which waited for: 4 -> 0; matrix products, arithmetic and copies ran while one was open for 11% -> 10% of each run, Pallas kernels for 0% -> 33%
where the time goes in v1:
time: 150 us; the launch traced here: 149 us
  Pallas kernels  61.8 us (41%)
  local copies, waits for them, and re-layouts  43.3 us (29%)
  blocking collectives  24.7 us (16%)
  between operations  14.2 us (9%)
  other arithmetic  4.58 us (3%)
    pallas_call x1, Pallas kernels, factors(): pl.pallas_call(functools.partial(factors_kernel, n, t), out_shape=(jax.Sh...  49.8 us
    unnamed x78, local copies, waits for them, and re-layouts  41.9 us
    all_gather x2, blocking collectives, body(): lax.all_gather((w - step_size * momentum_beta * m).astype(BF16), 'dp', ax...  24.7 us
    pallas_call x1, Pallas kernels, update(): pl.pallas_call(update_kernel, grid=(n,), out_shape=out_shapes, in_specs=s...  12.1 us
    convert_element_type x4, other arithmetic, body(): (w - step_size * momentum_beta * m).astype(BF16)  4.58 us
  transfers between devices with their start and end apart: 2, of which 0 were waited for; matrix products, arithmetic and copies ran while one was open for 10% of the time, Pallas kernels for 33%

profile of v1, /device:TPU:0, one launch (start us, length us, event | category | flops | bytes accessed | tf_op | source)
XLA Modules:
  0.0 148.8 jit_solution(13936686698147669173)
XLA Ops:
  7.2 1.7 %subtract_convert_fusion = bf16[96,768]{1,0:T(8,128)(2,1)} fusion(f32[96,768]{1,0:T(8,128)} %refs_20_.1, f32[96,768]{1,0:T(8,128)} %refs_21_.1), kind=kLoop, calls=%fused_computation | loop fusion | flops 221184 | bytes 737280 | tf_op jit(solution)/shard_map/convert_element_type | solution.py:333
  9.1 1.7 %subtract_convert_fusion.1 = bf16[96,768]{1,0:T(8,128)(2,1)} fusion(f32[96,768]{1,0:T(8,128)} %refs_10_.2, f32[96,768]{1,0:T(8,128)} %refs_11_.2), kind=kLoop, calls=%fused_computation.1 | loop fusion | flops 221184 | bytes 737280 | tf_op jit(solution)/shard_map/convert_element_type | solution.py:333
  10.8 1.9 %copy.41.refs_4_ = f32[1,768,576]{2,1,0:T(8,128)S(1)} copy(f32[1,768,576]{1,2,0:T(8,128)} %param.21) | data formatting | bytes 3538944 | tf_op args[1]
  12.7 2.2 %copy.40.refs_0_ = bf16[1,768,576]{2,1,0:T(8,128)(2,1)S(1)} copy(bf16[1,768,576]{1,2,0:T(8,128)(2,1)} %param.20) | data formatting | bytes 1769472 | tf_op args[0]
  14.9 1.8 %copy.43.refs_9_ = f32[768,32]{1,0:T(8,128)} copy(f32[768,32]{0,1:T(8,128)} %param.32) | data formatting | bytes 196608 | tf_op args[12]
  16.7 1.8 %copy.44.refs_10_ = f32[768,32]{1,0:T(8,128)} copy(f32[768,32]{0,1:T(8,128)} %param.27) | data formatting | bytes 196608 | tf_op args[7]
  18.5 1.8 %copy.45.refs_11_ = f32[768,32]{1,0:T(8,128)} copy(f32[768,32]{0,1:T(8,128)} %param.37) | data formatting | bytes 196608 | tf_op args[17]
  20.4 1.8 %copy.42.refs_8_ = f32[576,32]{1,0:T(8,128)} copy(f32[576,32]{0,1:T(8,128)} %param.22) | data formatting | bytes 147456 | tf_op args[2]
  22.1 1.0 subtract_convert_fusion.3
  23.2 12.4 %all-gather.2 = bf16[192,768]{1,0:T(8,128)(2,1)} all-gather(bf16[24,768]{1,0:T(8,128)(2,1)S(1)} %subtract_convert_fusion.3), channel_id=4, replica_groups=mesh['dp'=8,'tensor'=4] {'dp'}, dimensions={0}, use_global_device_ids=true | all-gather | bytes 331776 | tf_op jit(solution)/shard_map/all_gather | solution.py:333
  35.7 12.3 %all-gather = bf16[768,576]{1,0:T(8,128)(2,1)} all-gather(bf16[96,576]{1,0:T(8,128)(2,1)S(1)} %subtract_convert_fusion.2), channel_id=2, replica_groups=mesh['dp'=8,'tensor'=4] {'dp'}, dimensions={0}, use_global_device_ids=true | all-gather | bytes 995328 | tf_op jit(solution)/shard_map/all_gather | solution.py:333
  48.0 1.7 %copy-done.2 = f32[1,768,768]{2,1,0:T(8,128)S(1)} copy-done((f32[1,768,768]{2,1,0:T(8,128)S(1)}, f32[1,768,768]{2,1,0:T(8,128)}, u32[]{:S(2)}) %copy-start.2) | copy-done | bytes 2359320
  49.6 1.7 %copy-done.3 = f32[1,768,768]{2,1,0:T(8,128)S(1)} copy-done((f32[1,768,768]{2,1,0:T(8,128)S(1)}, f32[1,768,768]{2,1,0:T(8,128)}, u32[]{:S(2)}) %copy-start.3) | copy-done | bytes 2359320
  51.3 1.3 copy-done.6
  52.6 1.0 copy-done.24
  53.6 1.0 copy-done.25
  54.6 1.0 copy-done.30
  55.5 1.0 copy-done.31
  56.5 49.8 %factors.1 = (bf16[768,256]{1,0:T(8,128)(2,1)S(1)}, bf16[192,256]{1,0:T(8,128)(2,1)S(1)}, f32[128,768]{1,0:T(8,128)S(1)}) custom-call(bf16[1,768,576]{2,1,0:T(8,128)(2,1)S(1)} %copy.40.refs_0_, bf16[1,768,768]{2,1,0:T(8,128)(2,1)S(1)} %copy-done.4, bf16[1,192,768]{2,1,0:T(8,128)(2,1)S(1)} %copy-done.31, bf16[1,768,768]{2,1,0:T(8,128)(2,1)S(1)} %copy-done.6, ...), custom_call_target="tpu_custom_call" | custom-call | flops 4000000000 | bytes 60000000 | tf_op jit(solution)/shard_map/factors/pallas_call | solution.py:239
  109.0 1.2 copy-done.1
  110.2 1.3 copy-done.5
  111.5 1.3 copy-done.7
  112.8 1.3 copy-done.8
  114.0 1.3 copy-done.9
  115.3 1.0 copy-done.10
  116.3 1.0 copy-done.11
  119.2 1.0 copy-done.14
  122.0 1.1 copy-done.22
  123.1 1.0 copy-done.27
  125.9 12.1 %update.1 = (f32[8,96,576]{2,1,0:T(8,128)S(1)}, f32[96,576]{1,0:T(8,128)}, f32[96,576]{1,0:T(8,128)}, bf16[8,96,576]{2,1,0:T(8,128)(2,1)S(1)}, f32[8,96,768]{2,1...) custom-call(bf16[8,96,256]{2,1,0:T(8,128)(2,1)S(1)} %bitcast.43, ...), custom_call_target="tpu_custom_call" | custom-call | tf_op jit(solution)/shard_map/update/pallas_call | solution.py:317
  139.0 1.7 %copy.48 = f32[1,768,576]{1,2,0:T(8,128)} copy(f32[1,768,576]{2,1,0:T(8,128)S(1)} %bitcast.35) | data formatting | bytes 3538944
  140.7 1.3 copy.49
  (62 shorter events, 9.6 us)
Async XLA Ops:
  7.2 101.8 %all-gather.9.cloned.1.call-start = ((), (), s32[]{:S(2)}) async-start(), calls=%async_computation.1 | async-start | bytes 1327104 | tf_op jit(solution)/shard_map/all_gather | solution.py:333
  9.0 100.0 %all-gather.7.cloned.1.call-start = ((), (), s32[]{:S(2)}) async-start(), calls=%async_computation | async-start | bytes 1327104 | tf_op jit(solution)/shard_map/all_gather | solution.py:333
  12.7 35.3 %copy-start = (f32[1,768,576]{2,1,0:T(8,128)}, f32[1,768,576]{2,1,0:T(8,128)S(1)}, u32[]{:S(2)}) copy-start(f32[1,768,576]{2,1,0:T(8,128)S(1)} %copy.41.refs_4_) | copy-start | bytes 5308420
  12.7 9.4 %copy-start.28 = (f32[24,768]{1,0:T(8,128)S(1)}, f32[24,768]{1,0:T(8,128)}, u32[]{:S(2)}) copy-start(f32[24,768]{1,0:T(8,128)} %refs_15_.1) | copy-start | bytes 221188
  12.7 22.9 %copy-start.15 = (f32[96,576]{1,0:T(8,128)S(1)}, f32[96,576]{1,0:T(8,128)}, u32[]{:S(2)}) copy-start(f32[96,576]{1,0:T(8,128)} %refs_5_.3) | copy-start | bytes 663556
  12.7 22.9 %copy-start.17 = (f32[96,576]{1,0:T(8,128)S(1)}, f32[96,576]{1,0:T(8,128)}, u32[]{:S(2)}) copy-start(f32[96,576]{1,0:T(8,128)} %refs_6_.3) | copy-start | bytes 663556
  22.1 25.8 %copy-start.4 = (bf16[1,768,768]{2,1,0:T(8,128)(2,1)S(1)}, bf16[1,768,768]{2,1,0:T(8,128)(2,1)}, u32[]{:S(2)}) copy-start(bf16[1,768,768]{2,1,0:T(8,128)(2,1)} %refs_1_.1) | copy-start | bytes 3538948
  22.1 25.8 %copy-start.21 = (f32[1,192,768]{2,1,0:T(8,128)S(1)}, f32[1,192,768]{2,1,0:T(8,128)}, u32[]{:S(2)}) copy-start(f32[1,192,768]{2,1,0:T(8,128)} %refs_6_.2) | copy-start | bytes 1769476
  22.1 25.8 %copy-start.23 = (f32[768,32]{1,0:T(8,128)S(1)}, f32[768,32]{1,0:T(8,128)}, u32[]{:S(2)}) copy-start(f32[768,32]{1,0:T(8,128)} %copy.43.refs_9_) | copy-start | bytes 294916
  48.0 1.7 %copy-start.2 = (f32[1,768,768]{2,1,0:T(8,128)S(1)}, f32[1,768,768]{2,1,0:T(8,128)}, u32[]{:S(2)}) copy-start(f32[1,768,768]{2,1,0:T(8,128)} %refs_5_.2) | copy-start | bytes 7077892
  49.6 1.7 %copy-start.3 = (f32[1,768,768]{2,1,0:T(8,128)S(1)}, f32[1,768,768]{2,1,0:T(8,128)}, u32[]{:S(2)}) copy-start(f32[1,768,768]{2,1,0:T(8,128)} %refs_7_.1) | copy-start | bytes 7077892
  51.3 1.3 copy-start.6
  52.6 1.0 copy-start.24
  53.6 1.0 copy-start.25
  54.6 1.0 copy-start.30
  55.5 1.0 copy-start.31
  56.5 52.5 %copy-start.29 = (f32[24,768]{1,0:T(8,128)S(1)}, f32[24,768]{1,0:T(8,128)}, u32[]{:S(2)}) copy-start(f32[24,768]{1,0:T(8,128)} %refs_16_.1) | copy-start | bytes 221188
  109.0 1.2 copy-start.1
  110.2 1.3 copy-start.5
  111.5 1.3 copy-start.7
  112.8 1.3 copy-start.8
  114.0 1.3 copy-start.9
  115.3 1.0 copy-start.10
  116.3 1.0 copy-start.11
  117.2 1.0 copy-start.12
  118.2 1.0 copy-start.13
  119.1 1.0 copy-start.14
  122.0 1.1 copy-start.22
  123.1 1.0 copy-start.27
  124.1 1.0 copy-start.32
  138.0 1.0 copy-start.19
  139.0 1.7 %copy-start.20 = (bf16[8,96,576]{2,1,0:T(8,128)(2,1)S(1)}, bf16[8,96,576]{2,1,0:T(8,128)(2,1)}, u32[]{:S(2)}) copy-start(bf16[8,96,576]{2,1,0:T(8,128)(2,1)} %copy-done.19) | copy-start | bytes 2654212
  (5 other events, 4.2 us)
Sparse Core Ops, SparseCore 0:
  10.5 27.1 all-gather.8
  40.1 24.0 all-gather.6

commit v2 on v1

--- a/solution.py
+++ b/solution.py
@@ -20,6 +20,7 @@
 F32 = jnp.float32
 BF16 = jnp.bfloat16
 HIGHEST = lax.Precision.HIGHEST
+VMEM_BYTES = 60 * 1024 * 1024
 
 
 def dot_high(a, b, dims=(((1,), (0,)), ((), ()))):
@@ -69,12 +70,21 @@
 
 
 def factors_kernel(n, t, *refs):
-    grads, errors, bases = refs[0:4], refs[4:8], refs[8:12]
-    normed_ref, normed_out_ref, factor_ref = refs[12:15]
-    gbuf, ebuf, merged, rhs = refs[15:19], refs[19:23], refs[23:27], refs[27]
-    part, recv_part, cross, gathered = refs[28:32]
-    fpart, recv_f, cross_f = refs[32:35]
-    in_sem, s1, r1, s2, r2, s3, r3, s4, r4, s5, r5, s6, r6 = refs[35:48]
+    refs = list(refs)
+
+    def take(count):
+        out = refs[:count]
+        del refs[:count]
+        return out
+
+    grads, errors, bases, weights, moments = (take(COUNT) for _ in range(5))
+    normed_ref, normed_out_ref, flipped_ref, factor_ref, early_in_ref = take(5)
+    early_refs = [None] + take(COUNT - 1)
+    gbuf, ebuf, bbuf, wbuf, mbuf, own, merged = (take(COUNT) for _ in range(7))
+    early_in, rhs, part, recv_part, cross, gathered, fpart, recv_f, cross_f, full_f = take(10)
+    in_sem, w_sem, a_send, a_recv, f_send, f_recv = take(6)
+    s1, r1, s2, r2, s3, r3, s4, r4, s5, r5, s6, r6 = take(12)
+    early_refs[0] = early_in
 
     me = lax.axis_index("dp")
     my_t = lax.axis_index("tensor")
@@ -84,15 +94,24 @@
     w = recv_f.shape[2]
     pieces = width // w
 
-    loads = []
+    loads, late = [], []
     for j in range(COUNT):
-        pair = (
-            pltpu.make_async_copy(grads[j].at[0], gbuf[j], in_sem.at[2 * j]),
-            pltpu.make_async_copy(errors[j].at[0], ebuf[j], in_sem.at[2 * j + 1]),
+        group = (
+            pltpu.make_async_copy(bases[j], bbuf[j], in_sem.at[j, 0]),
+            pltpu.make_async_copy(grads[j].at[0], gbuf[j], in_sem.at[j, 1]),
+            pltpu.make_async_copy(errors[j].at[0], ebuf[j], in_sem.at[j, 2]),
         )
-        for copy in pair:
+        for copy in group:
             copy.start()
-        loads.append(pair)
+        loads.append(group)
+    for j in range(COUNT):
+        group = (
+            pltpu.make_async_copy(weights[j], wbuf[j], w_sem.at[j, 0]),
+            pltpu.make_async_copy(moments[j], mbuf[j], w_sem.at[j, 1]),
+        )
+        for copy in group:
+            copy.start()
+        late.append(group)
 
     barrier = pltpu.get_barrier_semaphore()
     for d in range(1, n):
@@ -100,15 +119,41 @@
     for d in range(1, t):
         pl.semaphore_signal(barrier, inc=1, device_id={"tensor": lax.rem(my_t + d, t)}, device_id_type=MESH)
 
+    def remote(axis, peer, source, target, send, recv):
+        copy = pltpu.make_async_remote_copy(
+            src_ref=source, dst_ref=target, send_sem=send, recv_sem=recv,
+            device_id={axis: peer}, device_id_type=MESH)
+        copy.start()
+        return copy
+
     def exchange(axis, size, index, source, target, send, recv):
         out = []
         for d in range(1, size):
             peer = lax.rem(index + d, size)
-            copy = pltpu.make_async_remote_copy(
-                src_ref=source(peer), dst_ref=target(d), send_sem=send.at[d - 1], recv_sem=recv.at[d - 1],
-                device_id={axis: peer}, device_id_type=MESH)
-            copy.start()
-            out.append(copy)
+            out.append(remote(axis, peer, source(peer), target(d), send.at[d - 1], recv.at[d - 1]))
+        return out
+
+    chips = n // 2
+    sibling = me + 1 - 2 * lax.rem(me, 2)
+
+    def early_start(j):
+        for copy in late[j]:
+            copy.wait()
+        own[j][...] = (wbuf[j][...] - (step_size * momentum_beta) * mbuf[j][...]).astype(BF16)
+        keep = pltpu.make_async_copy(own[j], early_refs[j].at[me], w_sem.at[j, 2])
+        keep.start()
+        out = [remote("dp", sibling, own[j], early_refs[j].at[me], a_send.at[j, 0], a_recv.at[j, 0])]
+        for d in range(1, chips):
+            out.append(remote("dp", lax.rem(me + 2 * d, n), own[j], early_refs[j].at[me],
+                              a_send.at[j, d], a_recv.at[j, d]))
+        return keep, out
+
+    def early_forward(j, copies):
+        out = []
+        for d in range(1, chips):
+            copies[d].wait_recv()
+            origin = early_refs[j].at[lax.rem(me - 2 * d + n, n)]
+            out.append(remote("dp", sibling, origin, origin, f_send.at[j, d - 1], f_recv.at[j, d - 1]))
         return out
 
     def rows_of(peer):
@@ -120,16 +165,21 @@
         return (pl.ds(pl.multiple_of((peer // pieces) * rc, 8), rc),
                 pl.ds(pl.multiple_of(lax.rem(peer, pieces) * w, 128), w))
 
-    part[...] = jnp.zeros_like(part)
-    for j in range(COUNT):
-        depth = bases[j].shape[0]
-        columns = [jnp.zeros((depth, RANK), F32)] * COUNT
-        columns[j] = bases[j][...]
-        hi, lo = split(jnp.concatenate(columns, axis=1))
+    for copy in loads[0]:
+        copy.wait()
+    merged[0][...] = (gbuf[0][...].astype(F32) + ebuf[0][...]).astype(BF16)
+    both = jnp.dot(jnp.concatenate(split(bbuf[0][...]), axis=0), merged[0][...], preferred_element_type=F32)
+    term = both[0:RANK] + both[RANK:]
+    part[...] = jnp.concatenate([term, jnp.zeros((LANES - RANK, rows), F32)], axis=0).T
+    for j in range(1, COUNT):
+        depth = bases[j].shape[1]
+        for copy in loads[j]:
+            copy.wait()
+        columns = [jnp.zeros((RANK, depth), F32)] * COUNT
+        columns[j] = bbuf[j][...]
+        hi, lo = split(jnp.concatenate(columns, axis=0).T)
         rhs[0:depth, 0:LANES] = hi
         rhs[0:depth, LANES:2 * LANES] = lo
-        for copy in loads[j]:
-            copy.wait()
         height = gbuf[j].shape[0]
         step = min(height, 192)
 
@@ -146,6 +196,8 @@
     pl.semaphore_wait(barrier, n - 1 + t - 1)
 
     first = exchange("dp", n, me, lambda p: part.at[rows_of(p), :], lambda d: recv_part.at[d - 1], s1, r1)
+    keeps, sent, forwarded = {}, {}, {}
+    keeps[0], sent[0] = early_start(0)
     chunk = part[rows_of(me), :]
     for d in range(1, n):
         first[d - 1].wait_recv()
@@ -166,6 +218,9 @@
     third = exchange("dp", n, me, lambda p: gathered.at[me], lambda d: gathered.at[me], s3, r3)
     for copy in third:
         copy.wait_recv()
+    for j in range(1, COUNT):
+        keeps[j], sent[j] = early_start(j)
+    forwarded[0] = early_forward(0, sent[0])
     compact = gathered[0, h:h + RANK, :]
     for k in range(1, n):
         compact = compact + gathered[k, h:h + RANK, :]
@@ -179,9 +234,14 @@
     normed_out_ref[:, 0:LANES] = hi[0:out_rows]
     normed_out_ref[:, LANES:2 * LANES] = lo[0:out_rows]
     flipped_hi, flipped_lo = split(normed.T)
-
+    flipped_ref[0:LANES, :] = flipped_hi
+    flipped_ref[LANES:2 * LANES, :] = flipped_lo
+
+    both = jnp.dot(merged[0][...], jnp.concatenate([hi, lo], axis=1), preferred_element_type=F32)
+    depth = merged[0].shape[0]
     fpart[...] = jnp.zeros_like(fpart)
-    for j in range(COUNT):
+    fpart[0:RANK, 0:depth] = (both[:, :LANES] + both[:, LANES:]).T[0:RANK]
+    for j in range(1, COUNT):
         height, depth = merged[j].shape
         both = jnp.concatenate(
             [flipped_hi[j * RANK:(j + 1) * RANK, 0:height], flipped_lo[j * RANK:(j + 1) * RANK, 0:height]], axis=0)
@@ -202,28 +262,49 @@
     for k in range(1, t):
         total_f = total_f + cross_f[k]
     row_part = (me // pieces) * rc >= COLS
-    factor_ref[piece_of(me)] = jnp.where(row_part, total_f, piece)
-    sixth = exchange("dp", n, me, lambda p: factor_ref.at[piece_of(me)], lambda d: factor_ref.at[piece_of(me)], s6, r6)
+    full_f[piece_of(me)] = jnp.where(row_part, total_f, piece)
+    sixth = exchange("dp", n, me, lambda p: full_f.at[piece_of(me)], lambda d: full_f.at[piece_of(me)], s6, r6)
+    for j in range(1, COUNT):
+        forwarded[j] = early_forward(j, sent[j])
+    keeps[0].wait()
+    sent[0][0].wait_recv()
+    for copy in forwarded[0]:
+        copy.wait_recv()
+    early_in_ref[...] = early_in[...].astype(F32).reshape(rows, early_in.shape[2]).T.astype(BF16)
     for copy in sixth:
         copy.wait_recv()
-    for group in (first, second, third, fourth, fifth, sixth):
+    factor_ref[...] = full_f[...]
+    for j in range(1, COUNT):
+        keeps[j].wait()
+        sent[j][0].wait_recv()
+        for copy in forwarded[j]:
+            copy.wait_recv()
+    groups = [first, second, third, fourth, fifth, sixth]
+    groups += [sent[j] for j in range(COUNT)] + [forwarded[j] for j in range(COUNT)]
+    for group in groups:
         for copy in group:
             copy.wait_send()
 
 
-def factors(n, t, grads, errors, bases):
-    rows = max(g.shape[1] for g in grads)
-    width = max(g.shape[2] for g in grads)
+def factors(n, t, grads, errors, bases, weights, moments):
+    rows = max(g.shape[1] for g in grads[1:])
+    width = max(g.shape[2] for g in grads[1:])
     h = rows // n
     rc = max(8, LANES // n)
     pieces = n * rc // LANES
     w = width // pieces
     out_rows = grads[2].shape[1]
     dma = pltpu.SemaphoreType.DMA
+    own = [x.shape for x in weights]
+    early = [(n,) + shape for shape in own]
     scratch = [pltpu.VMEM(g.shape[1:], BF16) for g in grads]
     scratch += [pltpu.VMEM(g.shape[1:], F32) for g in grads]
+    scratch += [pltpu.VMEM(g.shape, F32) for g in bases]
+    scratch += [pltpu.VMEM(shape, F32) for shape in own + own]
+    scratch += [pltpu.VMEM(shape, BF16) for shape in own]
     scratch += [pltpu.VMEM(g.shape[1:], BF16) for g in grads]
     scratch += [
+        pltpu.VMEM(early[0], BF16),
         pltpu.VMEM((width, 2 * LANES), BF16),
         pltpu.VMEM((rows, LANES), F32),
         pltpu.VMEM((n - 1, h, LANES), F32),
@@ -232,30 +313,36 @@
         pltpu.VMEM((LANES, width), F32),
         pltpu.VMEM((n - 1, rc, w), F32),
         pltpu.VMEM((t, rc, w), F32),
-        dma((2 * COUNT,)),
+        pltpu.VMEM((LANES, width), F32),
+        dma((COUNT, 3)), dma((COUNT, 3)),
+        dma((COUNT, n // 2)), dma((COUNT, n // 2)),
+        dma((COUNT, n // 2 - 1)), dma((COUNT, n // 2 - 1)),
     ]
     for size in (n, t, n, n, t, n):
         scratch += [dma((size - 1,)), dma((size - 1,))]
+    anywhere = pl.BlockSpec(memory_space=pl.ANY)
     return pl.pallas_call(
         functools.partial(factors_kernel, n, t),
-        out_shape=(
+        out_shape=[
             jax.ShapeDtypeStruct((rows, 2 * LANES), BF16),
             jax.ShapeDtypeStruct((out_rows, 2 * LANES), BF16),
+            jax.ShapeDtypeStruct((2 * LANES, rows), BF16),
             jax.ShapeDtypeStruct((LANES, width), F32),
-        ),
-        in_specs=[pl.BlockSpec(memory_space=pl.ANY)] * 8 + [pl.BlockSpec(memory_space=pltpu.VMEM)] * 4,
-        out_specs=[pl.BlockSpec(memory_space=pltpu.VMEM)] * 3,
+            jax.ShapeDtypeStruct((own[0][1], rows), BF16),
+        ] + [jax.ShapeDtypeStruct(shape, BF16) for shape in early[1:]],
+        in_specs=[anywhere] * (5 * COUNT),
+        out_specs=[pl.BlockSpec()] * 5 + [anywhere] * (COUNT - 1),
         scratch_shapes=scratch,
         compiler_params=pltpu.CompilerParams(
-            collective_id=0, has_side_effects=True, vmem_limit_bytes=40 * 1024 * 1024),
+            collective_id=0, has_side_effects=True, vmem_limit_bytes=VMEM_BYTES),
         cost_estimate=pl.CostEstimate(flops=4_000_000_000, bytes_accessed=60_000_000, transcendentals=0),
         name="factors",
-    )(*grads, *errors, *bases)
+    )(*grads, *errors, *bases, *weights, *moments)
 
 
 def update_kernel(*refs):
-    normed, normed_out, factor = refs[0:3]
-    ins, outs, rhs = refs[3:23], refs[23:39], refs[39]
+    normed, normed_out, flipped, factor = refs[0:4]
+    ins, outs, rhs, lhs_in = refs[4:24], refs[24:40], refs[40], refs[41]
     i = pl.program_id(0)
     me = lax.axis_index("dp")
 
@@ -267,25 +354,37 @@
             masked = jnp.where(block == j, value, jnp.zeros_like(value))
             rhs[j, 0:LANES, :] = masked
             rhs[j, LANES:2 * LANES, :] = masked
+        depth = lhs_in.shape[0] * lhs_in.shape[1]
+        turned = factor[:, 0:depth].T
+        turned = jnp.where(lane_block(turned.shape, 1) == 0, turned, 0.0)
+        turned = turned.reshape(lhs_in.shape[0], lhs_in.shape[1], LANES).astype(BF16)
+        lhs_in[:, :, 0:LANES] = turned
+        lhs_in[:, :, LANES:2 * LANES] = turned
 
     for j in range(COUNT):
         grad, error, weight, moment, early = ins[5 * j:5 * j + 5]
         residue, master, velocity, serving = outs[4 * j:4 * j + 4]
-        width = grad.shape[2]
         lhs = normed_out[0] if j == 2 else normed[0]
-        approx = jnp.dot(lhs, rhs[j, :, 0:width], preferred_element_type=F32)
+        factor_j = rhs.at[j, :, pl.ds(0, weight.shape[1])]
+        if j == 0:
+            approx = jnp.dot(lhs_in[i], flipped[...], preferred_element_type=F32)
+        else:
+            approx = jnp.dot(lhs, factor_j[...], preferred_element_type=F32)
         residue[0] = grad[0].astype(F32) + error[0] - approx
         serving[0] = (early[0].astype(F32) - step_size * approx).astype(BF16)
 
         @pl.when(i == me)
-        def _(weight=weight, moment=moment, master=master, velocity=velocity, approx=approx):
+        def _(j=j, weight=weight, moment=moment, master=master, velocity=velocity, approx=approx,
+              lhs=lhs, factor_j=factor_j):
+            if j == 0:
+                approx = jnp.dot(lhs, factor_j[...], preferred_element_type=F32)
             value = momentum_beta * moment[...] + approx
             velocity[...] = value
             master[...] = weight[...] - step_size * value
 
 
-def update(n, normed, normed_out, factor, groups):
-    def blocked(x, width=None):
+def update(n, normed, normed_out, flipped, factor, groups):
+    def blocked(x):
         x = x.reshape(n, -1, x.shape[-1])
         return x, pl.BlockSpec((1,) + x.shape[1:], lambda i: (i, 0, 0))
 
@@ -297,10 +396,10 @@
         x, spec = blocked(x)
         args.append(x)
         specs.append(spec)
-    args.append(factor)
-    specs.append(whole(factor.shape))
+    for x in (flipped, factor):
+        args.append(x)
+        specs.append(whole(x.shape))
     for grad, error, weight, moment, early in groups:
-        shapes = []
         for x in (grad, error):
             x, spec = blocked(x)
             args.append(x)
@@ -314,36 +413,39 @@
         out_shapes += [jax.ShapeDtypeStruct(blocks, F32), jax.ShapeDtypeStruct(weight.shape, F32),
                        jax.ShapeDtypeStruct(weight.shape, F32), jax.ShapeDtypeStruct(blocks, BF16)]
         out_specs += [spec, whole(weight.shape), whole(weight.shape), spec]
+    depth = groups[0][0].shape[1]
     return pl.pallas_call(
         update_kernel,
         grid=(n,),
         out_shape=out_shapes,
         in_specs=specs,
         out_specs=out_specs,
-        scratch_shapes=[pltpu.VMEM((COUNT, 2 * LANES, factor.shape[1]), BF16)],
-        compiler_params=pltpu.CompilerParams(vmem_limit_bytes=40 * 1024 * 1024),
+        scratch_shapes=[pltpu.VMEM((COUNT, 2 * LANES, factor.shape[1]), BF16),
+                        pltpu.VMEM((n, depth // n, 2 * LANES), BF16)],
+        compiler_params=pltpu.CompilerParams(vmem_limit_bytes=VMEM_BYTES),
         name="update",
     )(*args)
 
 
 def body(n, t, *args):
     inproj, outproj, expand, contract = (args[5 * k:5 * k + 5] for k in range(COUNT))
-    order = (inproj, expand, outproj, contract)
-    early = [
-        lax.all_gather((w - step_size * momentum_beta * m).astype(BF16), "dp", axis=0, tiled=False)
-        for _, _, _, w, m in order
-    ]
-    normed, normed_out, factor = factors(
-        n, t, [g[0] for g in order], [g[1] for g in order], [g[2] for g in order])
-    results = update(n, normed, normed_out, factor,
-                     [(g[0], g[1], g[3], g[4], u) for g, u in zip(order, early)])
+    order = [list(inproj), list(expand), list(outproj), list(contract)]
+    for k in (0, 1):
+        order[0][k] = order[0][k].transpose(0, 2, 1)
+    grads, errors, bases, weights, moments = (list(x) for x in zip(*order))
+    outputs = factors(n, t, grads, errors, [x.T for x in bases], weights, moments)
+    normed, normed_out, flipped, factor = outputs[0:4]
+    early = outputs[4:]
+    results = update(n, normed, normed_out, flipped, factor, list(zip(grads, errors, weights, moments, early)))
     outs = []
     for j in (0, 2, 1, 3):
-        grad = order[j][0]
+        grad = grads[j]
         height, width = grad.shape[1:]
         residue, master, velocity, serving = results[4 * j:4 * j + 4]
-        outs += [residue.reshape(grad.shape), factor[j * RANK:(j + 1) * RANK, 0:width].T,
-                 master, velocity, serving.reshape(height, width)]
+        residue, serving = residue.reshape(grad.shape), serving.reshape(height, width)
+        if j == 0:
+            residue, serving = residue.transpose(0, 2, 1), serving.T
+        outs += [residue, factor[j * RANK:(j + 1) * RANK, 0:master.shape[1]].T, master, velocity, serving]
     return tuple(outs)
 
 

time: 150 us -> 82.8 us (0.55)
  local copies, waits for them, and re-layouts: 43.3 us -> 1.36 us
  blocking collectives: 24.7 us -> 0 us
  Pallas kernels: 61.8 us -> 80.4 us
  between operations: 14.2 us -> 0.69 us
  other arithmetic: 4.58 us -> 0 us
    unnamed x78 -> x2, local copies, waits for them, and re-layouts: 41.9 us -> 0.01 us
    all_gather x2 -> x0, blocking collectives: 24.7 us -> none  [body(): lax.all_gather((w - step_size * momentum_beta * m).astype(BF16), 'dp', ax...]
    pallas_call x1, Pallas kernels: 49.8 us -> 64.4 us  [factors(): pl.pallas_call(functools.partial(factors_kernel, n, t), out_shape=[jax.Sh...]
    convert_element_type x4 -> x0, other arithmetic: 4.58 us -> none  [body(): (w - step_size * momentum_beta * m).astype(BF16)]
    pallas_call x1, Pallas kernels: 12.1 us -> 16.1 us  [update(): pl.pallas_call(update_kernel, grid=(n,), out_shape=out_shapes, in_specs=s...]
  transfers between devices with their start and end apart: 2 -> 0, of which waited for: 0 -> 0; matrix products, arithmetic and copies ran while one was open for 10% -> 0% of each run, Pallas kernels for 33% -> 0%
where the time goes in v2:
time: 82.8 us; the launch traced here: 82.5 us
  Pallas kernels  80.4 us (97%)
  local copies, waits for them, and re-layouts  1.36 us (2%)
    pallas_call x1, Pallas kernels, factors(): pl.pallas_call(functools.partial(factors_kernel, n, t), out_shape=[jax.Sh...  64.4 us
    pallas_call x1, Pallas kernels, update(): pl.pallas_call(update_kernel, grid=(n,), out_shape=out_shapes, in_specs=s...  16.1 us

profile of v2, /device:TPU:0, one launch (start us, length us, event | category | flops | bytes accessed | tf_op | source)
XLA Modules:
  0.0 82.5 jit_solution(2154268654005251692)
XLA Ops:
  0.7 64.4 %factors.1 = (bf16[768,256]{1,0:T(8,128)(2,1)}, bf16[192,256]{1,0:T(8,128)(2,1)}, bf16[256,768]{1,0:T(8,128)(2,1)}, f32[128,768]{1,0:T(8,128)}, bf16[576,768]{1,...) custom-call(bf16[1,576,768]{2,1,0:T(8,128)(2,1)} %bitcast.45, ...), custom_call_target="tpu_custom_call" | custom-call | flops 4000000000 | bytes 60000000 | tf_op jit(solution)/shard_map/factors/pallas_call | solution.py:324
  65.0 0.0 copy-start
  65.0 16.1 %update.1 = (f32[8,72,768]{2,1,0:T(8,128)}, f32[96,576]{1,0:T(8,128)}, f32[96,576]{1,0:T(8,128)}, bf16[8,72,768]{2,1,0:T(8,128)(2,1)}, f32[8,96,768]{2,1,0:T(8,1...) custom-call(bf16[8,96,256]{2,1,0:T(8,128)(2,1)} %bitcast.49, ...), custom_call_target="tpu_custom_call" | custom-call | tf_op jit(solution)/shard_map/update/pallas_call | solution.py:417
  81.1 0.0 copy-done
  81.1 0.7 slice_bitcast_fusion
  81.8 0.6 slice_bitcast_fusion.3
Async XLA Ops:
  65.0 16.1 %copy-start = (f32[128,768]{1,0:T(8,128)S(1)}, f32[128,768]{1,0:T(8,128)}, u32[]{:S(2)}) copy-start(f32[128,768]{1,0:T(8,128)} %get-tuple-element.47.refs_3_) | copy-start | bytes 1179652
